TPU v7x, 32 devices: a whole 2x2x4 slice. The times are simulated.
32 devices in a mesh: grp: 4 (over x, core), ops: 8 (over z, y).
Axes of the slice: x: 2, y: 2, z: 4, core: 2. Of those that a mesh axis runs over, the one named last changes fastest.
Arguments:
- psi: bfloat16 [28, 384, 384], P('grp', 'ops'), may hold values from -6 to 6
- left_ops: bfloat16 [28, 8, 384, 384], P('grp', 'ops'), may hold values from -1 to 2
- right_ops: bfloat16 [28, 8, 384, 384], P('grp', 'ops'), may hold values from -1 to 2
- right_group: int32 [28, 1], replicated, may hold values from 0 to 3; in each aligned block of 7 rows (0 to 6, 7 to 13, ...) at most 2 rows name the same one
- right_slot: int32 [28], replicated, may hold values from 0 to 6
- precond_diag: float32 [28, 384, 384], P('grp', 'ops'), may hold values from 0.25 to 8
Outputs:
- sigma: float32 [28, 384, 384], P('grp', 'ops')
- correction: float32 [28, 384, 384], P('grp', 'ops')
Inputs may be any that keep to these rules, and one draw needn't show every extreme that they name: In the 7 sectors of one group, at most 2 have their right_group equal to any one group; some group reaches 2.
All inputs are finite; a program needn't handle non-finite values.
Results may differ from a plain program's by a relative error of at most 0.0006.
The roundings to bfloat16 on the way count: a program that leaves them out, or rounds other values in their place, can miss the bound.
Values may be sent and summed in bfloat16 or wider, within the bound.
A program may use at most 64 MiB of HBM per device.

v0:
```python
import jax
import jax.numpy as jnp
from jax import lax
from jax.sharding import PartitionSpec as P


def early_sums(whole, partial_value, wave):
    whole_wave = whole.astype(jnp.float32)
    return lax.psum((jnp.sum(whole_wave * partial_value), jnp.sum(wave * wave)), ("grp", "ops"))


def shards(psi, left_ops, right_ops, right_group, right_slot, precond_diag):
    groups = lax.axis_size("grp")
    here = lax.axis_index("grp")
    spg = psi.shape[0]
    cap = (spg + groups - 1) // groups
    owner = right_group[:, 0].reshape(groups, spg)
    slots = right_slot.reshape(groups, spg)
    match = owner == here
    rank = jnp.cumsum(match.astype(jnp.int32), axis=1) - 1
    places = jnp.arange(cap, dtype=jnp.int32)
    pick = match[:, None, :] & (rank[:, None, :] == places[None, :, None])
    source = jnp.sum(jnp.where(pick, slots[:, None, :], 0), axis=2).reshape(-1)
    mine = lax.dynamic_index_in_dim(owner, here, 0, keepdims=False)
    order_ids = jnp.arange(spg, dtype=jnp.int32)
    earlier = (mine[:, None] == mine[None, :]) & (order_ids[None, :] < order_ids[:, None])
    position = mine * cap + jnp.sum(earlier.astype(jnp.int32), axis=1)
    whole = lax.all_gather(psi, "ops", axis=1, tiled=True)
    outgoing = jnp.take(right_ops, source, axis=0)
    incoming = lax.all_to_all(outgoing, "grp", split_axis=0, concat_axis=0, tiled=True)
    partner_blocks = jnp.take(incoming, position, axis=0)
    images = jnp.einsum(
        "jac,jkdc->jkad", whole, partner_blocks, preferred_element_type=jnp.float32
    ).astype(jnp.bfloat16)
    wave = psi.astype(jnp.float32)
    partial_value = jnp.einsum(
        "jkab,jkbd->jad", left_ops, images, preferred_element_type=jnp.float32
    )
    correlation, norm_sq = early_sums(whole, partial_value, wave)
    sigma = lax.psum_scatter(partial_value, "ops", scatter_dimension=1, tiled=True)
    theta = correlation / norm_sq
    gap = precond_diag - theta
    correction = (sigma - theta * wave) * gap / (gap * gap + 1.0)
    return (sigma, correction)


def solution(mesh):
    in_specs = (
        P("grp", "ops", None),
        P("grp", "ops", None, None),
        P("grp", "ops", None, None),
        P(),
        P(),
        P("grp", "ops", None),
    )
    out_specs = (P("grp", "ops", None), P("grp", "ops", None))
    return jax.shard_map(shards, mesh=mesh, in_specs=in_specs, out_specs=out_specs, check_vma=False)
```

profile of v0, /device:TPU:0, one launch (start us, length us, event | category | flops | bytes accessed | tf_op | source)
XLA Modules:
  0.0 167.5 jit_solution(9786601131466367111)
XLA Ops:
  7.2 0.0 copy-start
  7.2 0.0 all-gather.2.cloned.1.call-start
  7.2 0.7 all-gather.2.cloned.1.call-update
  7.9 0.5 broadcast.135
  8.4 1.3 reduce.3
  9.7 0.1 reshape_squeeze.3
  9.8 0.2 reduce_window_sum.11
  10.0 0.7 broadcast_in_dim.42
  10.8 0.1 select_reduce_fusion
  10.9 0.1 copy.11
  11.0 0.1 reshape.119
  11.1 0.1 reshape.118
  11.2 0.0 copy-done
  11.2 2.3 %gather_fusion = bf16[8,384,384]{2,1,0:T(8,128)(2,1)} fusion(bf16[7,384,384]{2,1,0:T(8,128)(2,1)S(1)} %bitcast.36, s32[1024]{0:T(1024)S(1)} %pad_clamp_fusion.1), kind=kCustom, calls=%fused_computation | custom fusion | bytes 4718624 | tf_op jit(solution)/shard_map/jit(_take)/gather | solution.py:29
  13.5 3.4 %bitcast_select_fusion = bf16[8,1,384,384]{3,2,1,0:T(8,128)(2,1)} fusion(bf16[8,384,384]{2,1,0:T(8,128)(2,1)} %gather_fusion, pred[8]{0:T(512)(128)(4,1)S(1)} %compare_and_fusion), kind=kLoop, calls=%fused_computation.3 | loop fusion | flops 1179648 | bytes 4718600 | tf_op jit(solution)/shard_map/jit(_take)/select_n | solution.py:29
  16.9 4.5 %all-to-all-start = ((bf16[8,1,384,384]{3,2,1,0:T(8,128)(2,1)}), bf16[8,1,384,384]{3,2,1,0:T(8,128)(2,1)}, u32[]{:S(2)}, u32[]{:S(2)}) async-start(bf16[8,1,384,384]{3,2,1,0:T(8,128)(2,1)} %bitcast_select_fusion), calls=%async_computation | async-start | bytes 4718592 | tf_op jit(solution)/shard_map/all_to_all | solution.py:30
  21.4 0.0 reduce-scatter.2.cloned.1.call-start
  21.4 0.2 convert_reduce_fusion
  21.7 28.9 %all-to-all-done = bf16[8,1,384,384]{3,2,1,0:T(8,128)(2,1)} async-done(((bf16[8,1,384,384]{3,2,1,0:T(8,128)(2,1)}), bf16[8,1,384,384]{3,2,1,0:T(8,128)(2,1)}, u32[]{:S(2)}, u32[]{:S(2)}) %all-to-all-start) | async-done | bytes 2359328 | tf_op jit(solution)/shard_map/all_to_all | solution.py:30
  50.6 4.0 %gather_fusion.1 = bf16[7,384,384]{2,1,0:T(8,128)(2,1)} fusion(bf16[8,384,384]{2,1,0:T(8,128)(2,1)} %bitcast.4, s32[1024]{0:T(1024)S(1)} %pad_clamp_fusion), kind=kCustom, calls=%fused_computation.1 | custom fusion | bytes 4128796 | tf_op jit(solution)/shard_map/jit(_take)/gather | solution.py:31
  54.6 7.1 %all-gather.2.cloned.1.call-done = bf16[7,384,384]{2,1,0:T(8,128)(2,1)} async-done(((bf16[7,48,384]{2,1,0:T(8,128)(2,1)}), bf16[7,384,384]{2,1,0:T(8,128)(2,1)}) %all-gather.2.cloned.1.call-update) | async-done | bytes 2064400 | tf_op jit(solution)/shard_map/all_gather | solution.py:28
  61.7 8.8 %multiply_reduce_fusion = (f32[]{:T(128)}, f32[7,384,384]{2,1,0:T(8,128)}) fusion(bf16[7,384,384]{2,1,0:T(8,128)(2,1)} %all-gather.2.cloned.1.call-done, bf16[7,1,384,384]{3,2,1,0:T(8,128)(2,1)} %param.7, bf16[7,384,384]{2,1,0:T(8,128)(2,1)} %gather_fusion.1, pred[7]{0:T(512)(128)(4,1)S(1)} %compare_and_fusion.1), kind=kOutput, calls=%fused_computation.2 | convolution fusion | flops 1590607872 | bytes 10321931 | tf_op jit(solution)/shard_map/jkab,jkbd->jad/dot_general | solution.py:36
  70.5 0.0 copy-start.1
  70.5 0.0 copy-start.2
  70.5 0.0 reduce-scatter.2.cloned.1.call-update
  70.5 0.9 copy-done.1
  71.5 0.8 fusion.11
  72.2 42.0 %all-reduce = (f32[]{:T(128)}, f32[]{:T(128)}) all-reduce(f32[]{:T(128)} %get-tuple-element.6, f32[]{:T(128)} %fusion.11), channel_id=1, replica_groups=mesh['grp'=4,'ops'=8] {'grp','ops'}, use_global_device_ids=true, to_apply=%region_5.6 | all-reduce | flops 2 | bytes 16 | tf_op jit(solution)/shard_map/psum | solution.py:9
  115.6 43.1 %reduce-scatter.2.cloned.1.call-done = f32[7,48,384]{2,1,0:T(8,128)} async-done(((f32[7,384,384]{2,1,0:T(8,128)}), f32[7,48,384]{2,1,0:T(8,128)}) %reduce-scatter.2.cloned.1.call-update) | async-done | bytes 516112 | tf_op jit(solution)/shard_map/reduce_scatter | solution.py:40
  158.7 0.0 copy-done.2
  158.7 2.0 %fusion.14 = f32[7,48,384]{2,1,0:T(8,128)} fusion(f32[7,48,384]{2,1,0:T(8,128)} %reduce-scatter.2.cloned.1.call-done, bf16[7,48,384]{2,1,0:T(8,128)(2,1)S(1)} %copy-done.1, f32[7,48,384]{2,1,0:T(8,128)S(1)} %copy-done.2, f32[]{:T(128)S(6)} %div.6), kind=kLoop, calls=%fused_computation.17 | loop fusion | flops 1032192 | bytes 1806340 | tf_op jit(solution)/shard_map/div | solution.py:43
  (9 shorter events, 0.1 us)
Async XLA Ops:
  7.2 4.0 %copy-start = (bf16[7,1,384,384]{3,2,1,0:T(8,128)(2,1)S(1)}, bf16[7,1,384,384]{3,2,1,0:T(8,128)(2,1)}, u32[]{:S(2)}) copy-start(bf16[7,1,384,384]{3,2,1,0:T(8,128)(2,1)} %param.8) | copy-start | bytes 6193156
  7.2 54.5 %all-gather.2.cloned.1.call-start = ((), (), s32[]{:S(2)}) async-start(), calls=%async_computation.2 | async-start | bytes 2322432 | tf_op jit(solution)/shard_map/all_gather | solution.py:28
  16.9 33.7 %all-to-all-start = ((bf16[8,1,384,384]{3,2,1,0:T(8,128)(2,1)}), bf16[8,1,384,384]{3,2,1,0:T(8,128)(2,1)}, u32[]{:S(2)}, u32[]{:S(2)}) async-start(bf16[8,1,384,384]{3,2,1,0:T(8,128)(2,1)} %bitcast_select_fusion), calls=%async_computation | async-start | bytes 4718592 | tf_op jit(solution)/shard_map/all_to_all | solution.py:30
  21.4 137.3 %reduce-scatter.2.cloned.1.call-start = ((), (), s32[]{:S(2)}) async-start(), calls=%async_computation.3 | async-start | bytes 4644864 | tf_op jit(solution)/shard_map/reduce_scatter | solution.py:40
  70.5 0.9 copy-start.1
  70.5 88.1 %copy-start.2 = (f32[7,48,384]{2,1,0:T(8,128)S(1)}, f32[7,48,384]{2,1,0:T(8,128)}, u32[]{:S(2)}) copy-start(f32[7,48,384]{2,1,0:T(8,128)} %param.11) | copy-start | bytes 1548292
Sparse Core Ops, SparseCore 0:
  10.2 51.4 all-gather.1
  70.7 87.9 reduce-scatter.1
where the time goes:
time: 168 us; the launch traced here: 167 us
  waiting for transfers between devices  79.8 us (48%)
  blocking collectives  42 us (25%)
  between operations  15.4 us (9%)
  matrix products  8.82 us (5%)
  local copies, waits for them, and re-layouts  8.78 us (5%)
  other arithmetic  8.06 us (5%)
  starting transfers between devices  4.56 us (3%)
    reduce_scatter x1, waiting for transfers between devices, shards(): lax.psum_scatter(partial_value, 'ops', scatter_dimension=1, tiled=True)  43.1 us
    psum x1, blocking collectives, early_sums(): lax.psum((jnp.sum(whole_wave * partial_value), jnp.sum(wave * wave)), ('g...  42 us
    all_to_all x1, waiting for transfers between devices, shards(): lax.all_to_all(outgoing, 'grp', split_axis=0, concat_axis=0, tiled=True)  28.9 us
    dot_general x1, matrix products, shards(): jnp.einsum('jkab,jkbd->jad', left_ops, images, preferred_element_type=jnp...  8.82 us
    all_gather x1, waiting for transfers between devices, shards(): whole = lax.all_gather(psi, 'ops', axis=1, tiled=True)  7.1 us
    all_to_all x1, starting transfers between devices, shards(): lax.all_to_all(outgoing, 'grp', split_axis=0, concat_axis=0, tiled=True)  4.49 us
    gather x1, local copies, waits for them, and re-layouts, shards(): partner_blocks = jnp.take(incoming, position, axis=0)  3.97 us
    select_n x2, other arithmetic, shards(): outgoing = jnp.take(right_ops, source, axis=0)  3.39 us
  transfers between devices with their start and end apart: 3, of which 3 were waited for; matrix products, arithmetic and copies ran while one was open for 8% of the time, Pallas kernels for 0%

commit v1 on v0

--- a/solution.py
+++ b/solution.py
@@ -1,7 +1,14 @@
+import functools
+
 import jax
 import jax.numpy as jnp
 from jax import lax
+from jax.experimental import pallas as pl
+from jax.experimental.pallas import tpu as pltpu
 from jax.sharding import PartitionSpec as P
+
+MESH = pl.DeviceIdType.MESH
+VMEM_BYTES = 60 * 1024 * 1024
 
 
 def early_sums(whole, partial_value, wave):
@@ -9,7 +16,7 @@
     return lax.psum((jnp.sum(whole_wave * partial_value), jnp.sum(wave * wave)), ("grp", "ops"))
 
 
-def shards(psi, left_ops, right_ops, right_group, right_slot, precond_diag):
+def plain_shards(psi, left_ops, right_ops, right_group, right_slot, precond_diag):
     groups = lax.axis_size("grp")
     here = lax.axis_index("grp")
     spg = psi.shape[0]
@@ -44,6 +51,261 @@
     return (sigma, correction)
 
 
+def chunks_of(spg):
+    cuts, at = [], 0
+    while at < spg:
+        size = min(2, spg - at) if spg - at != 3 else 3
+        cuts.append((at, size))
+        at += size
+    return cuts
+
+
+def fold(value):
+    rows, cols = value.shape
+    value = jnp.sum(value.reshape(rows // 8, 8, cols), axis=0)
+    total = value[:, 0:128]
+    for at in range(128, cols, 128):
+        total = total + value[:, at:at + 128]
+    return total
+
+
+def kernel(groups, n_z, n_y, cap, rg, rs, psi, left, right, diag, sig_o, cor_o,
+           whole, lv, rv, dv, rsend, rrecv, part, yrecv, zacc, zrecv, sigv, corv,
+           stat, statz, staty, statg, send_sem, recv_sem, local_sem):
+    spg, rows, sec = psi.shape
+    g = lax.axis_index("grp")
+    o = lax.axis_index("ops")
+    z, y = o // n_y, o % n_y
+    count = iter(range(1 << 20))
+    count_local = iter(range(1 << 20))
+    sent = []
+
+    def z_peer(d):
+        return {"ops": lax.rem(z + d, n_z) * n_y + y}
+
+    def z_from(d):
+        return lax.rem(z + n_z - d, n_z)
+
+    y_peer = {"ops": z * n_y + (n_y - 1 - y)}
+
+    def g_peer(d):
+        return {"grp": lax.rem(g + d, groups)}
+
+    def remote(src, dst, device, arrive=None):
+        i = next(count)
+        copy = pltpu.make_async_remote_copy(
+            src_ref=src, dst_ref=dst, send_sem=send_sem.at[i], recv_sem=recv_sem.at[i],
+            device_id=device, device_id_type=MESH)
+        copy.start()
+        sent.append(copy)
+        if arrive is None:
+            return copy
+        return pltpu.make_async_remote_copy(
+            src_ref=src, dst_ref=arrive, send_sem=send_sem.at[i], recv_sem=recv_sem.at[i],
+            device_id=device, device_id_type=MESH)
+
+    def local(src, dst):
+        copy = pltpu.make_async_copy(src, dst, local_sem.at[next(count_local)])
+        copy.start()
+        return copy
+
+    def rows_of(owner):
+        return pl.ds(pl.multiple_of(owner * rows, rows), rows)
+
+    right_in = local(right.at[:, 0], rv)
+    psi_in = local(psi, whole.at[:, rows_of(o)])
+    left_in = local(left.at[:, 0], lv)
+    diag_in = local(diag, dv)
+
+    barrier = pltpu.get_barrier_semaphore()
+    peers = [z_peer(d) for d in range(1, n_z)] + [y_peer] + [g_peer(d) for d in range(1, groups)]
+    for peer in peers:
+        pl.semaphore_signal(barrier, inc=1, device_id=peer, device_id_type=MESH)
+    pl.semaphore_wait(barrier, len(peers))
+
+    from_z, from_y = {}, []
+    cuts = chunks_of(spg)
+    for c, (at, size) in enumerate(cuts):
+        src = psi.at[pl.ds(at, size)]
+        spot = whole.at[pl.ds(at, size), rows_of(o)]
+        from_y.append(remote(src, spot, y_peer,
+                             whole.at[pl.ds(at, size), rows_of(z * n_y + n_y - 1 - y)]))
+        for d in range(1, n_z):
+            from_z[c, d] = remote(src, spot, z_peer(d),
+                                  whole.at[pl.ds(at, size), rows_of(z_from(d) * n_y + y)])
+
+    right_in.wait()
+    for d in range(groups):
+        there = lax.rem(g + d, groups)
+        found = jnp.int32(0)
+        source = [jnp.int32(0)] * cap
+        for j in range(spg):
+            match = rg[there * spg + j, 0] == g
+            slot = rs[there * spg + j]
+            for r in range(cap):
+                source[r] = jnp.where(match & (found == r), slot, source[r])
+            found = found + match.astype(jnp.int32)
+        for r in range(cap):
+            if d == 0:
+                rrecv[r] = rv[source[r]]
+            else:
+                rsend[(d - 1) * cap + r] = rv[source[r]]
+    from_g = []
+    for r in range(cap):
+        for d in sorted(range(1, groups), key=lambda d: abs(2 * d - groups)):
+            from_g.append(remote(rsend.at[(d - 1) * cap + r], rrecv.at[d * cap + r], g_peer(d)))
+
+    for c, (at, size) in enumerate(cuts):
+        for d in range(1, n_z):
+            from_z[c, d].wait_recv()
+            owner = z_from(d) * n_y
+            spot = whole.at[pl.ds(at, size), rows_of(owner + y)]
+            from_y.append(remote(spot, spot, y_peer,
+                                 whole.at[pl.ds(at, size), rows_of(owner + n_y - 1 - y)]))
+
+    position = []
+    mine = [rg[g * spg + j, 0] for j in range(spg)]
+    for j in range(spg):
+        rank = jnp.int32(0)
+        for i in range(j):
+            rank = rank + (mine[i] == mine[j]).astype(jnp.int32)
+        position.append(lax.rem(g - mine[j] + groups, groups) * cap
+                        + jnp.minimum(rank, cap - 1))
+
+    psi_in.wait()
+    norm = jnp.zeros((8, 128), jnp.float32)
+    for j in range(spg):
+        wave = whole[j, rows_of(o), :].astype(jnp.float32)
+        norm = norm + fold(wave * wave)
+    stat[0, 1] = norm
+    left_in.wait()
+    for copy in from_g + from_y:
+        copy.wait_recv()
+
+    corr = jnp.zeros((8, 128), jnp.float32)
+    across = []
+    for j in range(spg):
+        block = whole[j]
+        image = lax.dot_general(block, rrecv[position[j]], (((1,), (1,)), ((), ())),
+                                preferred_element_type=jnp.float32).astype(jnp.bfloat16)
+        value = jnp.dot(lv[j], image, preferred_element_type=jnp.float32)
+        part[j] = value.reshape(n_z, n_y, rows, sec)
+        corr = corr + fold(block.astype(jnp.float32) * value)
+        across.append(remote(part.at[j, :, n_y - 1 - y], yrecv.at[j], y_peer))
+    stat[0, 0] = corr
+
+    def sums_out(stage):
+        if stage == 0:
+            return [remote(stat.at[0], statz.at[d - 1], z_peer(d)) for d in range(1, n_z)]
+        if stage == 1:
+            return [remote(stat.at[1], staty.at[0], y_peer)]
+        return [remote(stat.at[2], statg.at[d - 1], g_peer(d)) for d in range(1, groups)]
+
+    def sums_in(stage, copies):
+        landed = (statz, staty, statg)[stage]
+        for copy in copies:
+            copy.wait_recv()
+        total = stat[stage]
+        for i in range(landed.shape[0]):
+            total = total + landed[i]
+        stat[stage + 1] = total
+
+    sums = sums_out(0)
+    diag_in.wait()
+    along = []
+    outs = []
+    theta = None
+
+    def finish(j):
+        for copy in along[j]:
+            copy.wait_recv()
+        sigma = zacc[j, z]
+        for d in range(1, n_z):
+            sigma = sigma + zrecv[j, d - 1]
+        sigv[j] = sigma
+        outs.append(local(sigv.at[j], sig_o.at[j]))
+        wave = whole[j, rows_of(o), :].astype(jnp.float32)
+        gap = dv[j] - theta
+        corv[j] = (sigma - theta * wave) * gap / (gap * gap + 1.0)
+        outs.append(local(corv.at[j], cor_o.at[j]))
+
+    done = 0
+    for j in range(spg):
+        across[j].wait_recv()
+        for k in range(n_z):
+            zacc[j, k] = part[j, k, y] + yrecv[j, k]
+        along.append([remote(zacc.at[j, lax.rem(z + d, n_z)], zrecv.at[j, d - 1], z_peer(d))
+                      for d in range(1, n_z)])
+        if j < 3:
+            sums_in(j, sums)
+            if j < 2:
+                sums = sums_out(j + 1)
+            else:
+                theta = jnp.sum(stat[3, 0]) / jnp.sum(stat[3, 1])
+        elif j >= 4:
+            finish(done)
+            done += 1
+    while done < spg:
+        finish(done)
+        done += 1
+    for copy in sent:
+        copy.wait_send()
+    for copy in outs:
+        copy.wait()
+
+
+def fused_shards(psi, left_ops, right_ops, right_group, right_slot, precond_diag):
+    groups = lax.axis_size("grp")
+    n_y = 2
+    n_z = lax.axis_size("ops") // n_y
+    spg, rows, sec = psi.shape
+    cap = (spg + groups - 1) // groups
+    f32, bf16 = jnp.float32, jnp.bfloat16
+    cuts = len(chunks_of(spg))
+    copies = cuts * (2 * n_z - 1) + (groups - 1) * cap + spg * n_z + (n_z - 1) + 1 + (groups - 1)
+    shape = jax.ShapeDtypeStruct((spg, rows, sec), f32)
+    return pl.pallas_call(
+        functools.partial(kernel, groups, n_z, n_y, cap),
+        out_shape=(shape, shape),
+        in_specs=[pl.BlockSpec(memory_space=pltpu.SMEM)] * 2 + [pl.BlockSpec(memory_space=pl.ANY)] * 4,
+        out_specs=(pl.BlockSpec(memory_space=pl.ANY),) * 2,
+        scratch_shapes=[
+            pltpu.VMEM((spg, sec, sec), bf16),
+            pltpu.VMEM((spg, sec, sec), bf16),
+            pltpu.VMEM((spg, sec, sec), bf16),
+            pltpu.VMEM((spg, rows, sec), f32),
+            pltpu.VMEM(((groups - 1) * cap, sec, sec), bf16),
+            pltpu.VMEM((groups * cap, sec, sec), bf16),
+            pltpu.VMEM((spg, n_z, n_y, rows, sec), f32),
+            pltpu.VMEM((spg, n_z, rows, sec), f32),
+            pltpu.VMEM((spg, n_z, rows, sec), f32),
+            pltpu.VMEM((spg, n_z - 1, rows, sec), f32),
+            pltpu.VMEM((spg, rows, sec), f32),
+            pltpu.VMEM((spg, rows, sec), f32),
+            pltpu.VMEM((4, 2, 8, 128), f32),
+            pltpu.VMEM((n_z - 1, 2, 8, 128), f32),
+            pltpu.VMEM((1, 2, 8, 128), f32),
+            pltpu.VMEM((groups - 1, 2, 8, 128), f32),
+            pltpu.SemaphoreType.DMA((copies,)),
+            pltpu.SemaphoreType.DMA((copies,)),
+            pltpu.SemaphoreType.DMA((4 + 2 * spg,)),
+        ],
+        compiler_params=pltpu.CompilerParams(
+            collective_id=0, has_side_effects=True, vmem_limit_bytes=VMEM_BYTES),
+    )(right_group, right_slot, psi, left_ops, right_ops, precond_diag)
+
+
+def shards(psi, left_ops, right_ops, right_group, right_slot, precond_diag):
+    spg, rows, sec = psi.shape
+    groups, ops = lax.axis_size("grp"), lax.axis_size("ops")
+    cap = (spg + groups - 1) // groups
+    held = sec * sec * (2 * (3 * spg + (2 * groups - 1) * cap) + 4 * (3 * spg))
+    fits = (rows % 16 == 0 and sec % 128 == 0 and ops % 2 == 0 and ops > 2 and groups > 1
+            and spg > 3 and left_ops.shape[1] == 1 and held < 40 * 1024 * 1024)
+    form = fused_shards if fits else plain_shards
+    return form(psi, left_ops, right_ops, right_group, right_slot, precond_diag)
+
+
 def solution(mesh):
     in_specs = (
         P("grp", "ops", None),

time: 168 us -> 121 us (0.72)
  Pallas kernels: 0 us -> 115 us
  waiting for transfers between devices: 79.8 us -> 0 us
  blocking collectives: 42 us -> 0 us
  between operations: 15.4 us -> 0.64 us
  matrix products: 8.82 us -> 0 us
  other arithmetic: 8.06 us -> 0 us
  starting transfers between devices: 4.56 us -> 0 us
  local copies, waits for them, and re-layouts: 8.78 us -> 5.06 us
    pallas_call x0 -> x1, Pallas kernels: none -> 115 us  [fused_shards(): pl.pallas_call(functools.partial(kernel, groups, n_z, n_y, cap), out_shap...]
    reduce_scatter x1 -> x0, waiting for transfers between devices: 43.1 us -> none  [shards(): lax.psum_scatter(partial_value, 'ops', scatter_dimension=1, tiled=True)]
    psum x1 -> x0, blocking collectives: 42 us -> none  [early_sums(): lax.psum((jnp.sum(whole_wave * partial_value), jnp.sum(wave * wave)), ('g...]
    all_to_all x1 -> x0, waiting for transfers between devices: 28.9 us -> none  [shards(): lax.all_to_all(outgoing, 'grp', split_axis=0, concat_axis=0, tiled=True)]
    dot_general x1 -> x0, matrix products: 8.82 us -> none  [shards(): jnp.einsum('jkab,jkbd->jad', left_ops, images, preferred_element_type=jnp...]
    all_gather x1 -> x0, waiting for transfers between devices: 7.1 us -> none  [shards(): whole = lax.all_gather(psi, 'ops', axis=1, tiled=True)]
    gather x2 -> x0, local copies, waits for them, and re-layouts: 6.24 us -> none  [the longest x1 3.97 us: shards(): partner_blocks = jnp.take(incoming, position, axis=0)]
    all_to_all x1 -> x0, starting transfers between devices: 4.49 us -> none  [shards(): lax.all_to_all(outgoing, 'grp', split_axis=0, concat_axis=0, tiled=True)]
  transfers between devices with their start and end apart: 3 -> 0, of which waited for: 3 -> 0; matrix products, arithmetic and copies ran while one was open for 8% -> 0% of each run, Pallas kernels for 0% -> 0%
where the time goes in v1:
time: 121 us; the launch traced here: 120 us
  Pallas kernels  115 us (95%)
  local copies, waits for them, and re-layouts  5.06 us (4%)
    pallas_call x1, Pallas kernels, fused_shards(): pl.pallas_call(functools.partial(kernel, groups, n_z, n_y, cap), out_shap...  115 us
    unnamed x3, local copies, waits for them, and re-layouts  5.06 us

profile of v1, /device:TPU:0, one launch (start us, length us, event | category | flops | bytes accessed | tf_op | source)
XLA Modules:
  0.0 120.4 jit_solution(15124571726350400772)
XLA Ops:
  0.6 1.3 %copy.8.rg = s32[28,1]{1,0:T(8,128)} copy(s32[28,1]{0,1:T(1,128)} %param.9) | data formatting | bytes 224 | tf_op args[3]
  2.0 114.7 %shard_map.77 = (f32[7,48,384]{2,1,0:T(8,128)}, f32[7,48,384]{2,1,0:T(8,128)}) custom-call(s32[28,1]{1,0:T(8,128)} %copy.8.rg, s32[28]{0:T(128)} %rs.1, bf16[7,48,384]{2,1,0:T(8,128)(2,1)} %psi.1, bf16[7,1,384,384]{3,2,1,0:T(8,128)(2,1)} %left.1, bf16[7,1,384,384]{3,2,1,0:T(8,128)(2,1)} %right.1, f32[7,48,384]{2,1,0:T(8,128)} %diag.1), custom_call_target="tpu_custom_call" | custom-call | tf_op jit(solution)/shard_map/pallas_call | solution.py:267
  116.6 1.9 %copy.11 = f32[7,48,384]{2,1,0:T(8,128)} copy(f32[7,48,384]{2,1,0:T(8,128)} %get-tuple-element.4) | data formatting | bytes 1032192
  118.5 1.9 %copy.12 = f32[7,48,384]{2,1,0:T(8,128)} copy(f32[7,48,384]{2,1,0:T(8,128)} %get-tuple-element.5) | data formatting | bytes 1032192

commit v2 on v1

--- a/solution.py
+++ b/solution.py
@@ -9,6 +9,8 @@
 
 MESH = pl.DeviceIdType.MESH
 VMEM_BYTES = 60 * 1024 * 1024
+AHEAD = 3
+LATE = 4
 
 
 def early_sums(whole, partial_value, wave):
@@ -140,7 +142,7 @@
         found = jnp.int32(0)
         source = [jnp.int32(0)] * cap
         for j in range(spg):
-            match = rg[there * spg + j, 0] == g
+            match = rg[there * spg + j] == g
             slot = rs[there * spg + j]
             for r in range(cap):
                 source[r] = jnp.where(match & (found == r), slot, source[r])
@@ -164,7 +166,7 @@
                                  whole.at[pl.ds(at, size), rows_of(owner + n_y - 1 - y)]))
 
     position = []
-    mine = [rg[g * spg + j, 0] for j in range(spg)]
+    mine = [rg[g * spg + j] for j in range(spg)]
     for j in range(spg):
         rank = jnp.int32(0)
         for i in range(j):
@@ -184,6 +186,10 @@
 
     corr = jnp.zeros((8, 128), jnp.float32)
     across = []
+
+    def y_out(j):
+        return remote(part.at[j, :, n_y - 1 - y], yrecv.at[j], y_peer)
+
     for j in range(spg):
         block = whole[j]
         image = lax.dot_general(block, rrecv[position[j]], (((1,), (1,)), ((), ())),
@@ -191,18 +197,19 @@
         value = jnp.dot(lv[j], image, preferred_element_type=jnp.float32)
         part[j] = value.reshape(n_z, n_y, rows, sec)
         corr = corr + fold(block.astype(jnp.float32) * value)
-        across.append(remote(part.at[j, :, n_y - 1 - y], yrecv.at[j], y_peer))
+        if j < AHEAD:
+            across.append(y_out(j))
     stat[0, 0] = corr
 
     def sums_out(stage):
         if stage == 0:
-            return [remote(stat.at[0], statz.at[d - 1], z_peer(d)) for d in range(1, n_z)]
+            return [remote(stat.at[0], statg.at[d - 1], g_peer(d)) for d in range(1, groups)]
         if stage == 1:
-            return [remote(stat.at[1], staty.at[0], y_peer)]
-        return [remote(stat.at[2], statg.at[d - 1], g_peer(d)) for d in range(1, groups)]
+            return [remote(stat.at[1], statz.at[d - 1], z_peer(d)) for d in range(1, n_z)]
+        return [remote(stat.at[2], staty.at[0], y_peer)]
 
     def sums_in(stage, copies):
-        landed = (statz, staty, statg)[stage]
+        landed = (statg, statz, staty)[stage]
         for copy in copies:
             copy.wait_recv()
         total = stat[stage]
@@ -232,17 +239,19 @@
     done = 0
     for j in range(spg):
         across[j].wait_recv()
+        if j < 2:
+            sums_in(j, sums)
+            sums = sums_out(j + 1)
+        elif j == LATE:
+            sums_in(2, sums)
+            theta = jnp.sum(stat[3, 0]) / jnp.sum(stat[3, 1])
+        if j + AHEAD < spg:
+            across.append(y_out(j + AHEAD))
         for k in range(n_z):
             zacc[j, k] = part[j, k, y] + yrecv[j, k]
         along.append([remote(zacc.at[j, lax.rem(z + d, n_z)], zrecv.at[j, d - 1], z_peer(d))
                       for d in range(1, n_z)])
-        if j < 3:
-            sums_in(j, sums)
-            if j < 2:
-                sums = sums_out(j + 1)
-            else:
-                theta = jnp.sum(stat[3, 0]) / jnp.sum(stat[3, 1])
-        elif j >= 4:
+        if j > LATE:
             finish(done)
             done += 1
     while done < spg:
@@ -292,7 +301,7 @@
         ],
         compiler_params=pltpu.CompilerParams(
             collective_id=0, has_side_effects=True, vmem_limit_bytes=VMEM_BYTES),
-    )(right_group, right_slot, psi, left_ops, right_ops, precond_diag)
+    )(right_group.reshape(-1), right_slot, psi, left_ops, right_ops, precond_diag)
 
 
 def shards(psi, left_ops, right_ops, right_group, right_slot, precond_diag):
@@ -301,7 +310,7 @@
     cap = (spg + groups - 1) // groups
     held = sec * sec * (2 * (3 * spg + (2 * groups - 1) * cap) + 4 * (3 * spg))
     fits = (rows % 16 == 0 and sec % 128 == 0 and ops % 2 == 0 and ops > 2 and groups > 1
-            and spg > 3 and left_ops.shape[1] == 1 and held < 40 * 1024 * 1024)
+            and spg > LATE and left_ops.shape[1] == 1 and held < 40 * 1024 * 1024)
     form = fused_shards if fits else plain_shards
     return form(psi, left_ops, right_ops, right_group, right_slot, precond_diag)
 

time: 121 us -> 96 us (0.79)
  Pallas kernels: 115 us -> 91.4 us
  local copies, waits for them, and re-layouts: 5.06 us -> 3.72 us
    pallas_call x1, Pallas kernels: 115 us -> 91.4 us  [fused_shards(): pl.pallas_call(functools.partial(kernel, groups, n_z, n_y, cap), out_shap...]
    unnamed x3 -> x2, local copies, waits for them, and re-layouts: 5.06 us -> 3.72 us
where the time goes in v2:
time: 96 us; the launch traced here: 95.8 us
  Pallas kernels  91.4 us (95%)
  local copies, waits for them, and re-layouts  3.72 us (4%)
    pallas_call x1, Pallas kernels, fused_shards(): pl.pallas_call(functools.partial(kernel, groups, n_z, n_y, cap), out_shap...  91.4 us
    unnamed x2, local copies, waits for them, and re-layouts  3.72 us

profile of v2, /device:TPU:0, one launch (start us, length us, event | category | flops | bytes accessed | tf_op | source)
XLA Modules:
  0.0 95.8 jit_solution(6205229706120345067)
XLA Ops:
  0.6 91.4 %shard_map.77 = (f32[7,48,384]{2,1,0:T(8,128)}, f32[7,48,384]{2,1,0:T(8,128)}) custom-call(s32[28]{0:T(128)} %bitcast.1, s32[28]{0:T(128)} %rs.1, bf16[7,48,384]{2,1,0:T(8,128)(2,1)} %psi.1, bf16[7,1,384,384]{3,2,1,0:T(8,128)(2,1)} %left.1, bf16[7,1,384,384]{3,2,1,0:T(8,128)(2,1)} %right.1, f32[7,48,384]{2,1,0:T(8,128)} %diag.1), custom_call_target="tpu_custom_call" | custom-call | tf_op jit(solution)/shard_map/pallas_call | solution.py:276
  92.0 1.9 %copy.10 = f32[7,48,384]{2,1,0:T(8,128)} copy(f32[7,48,384]{2,1,0:T(8,128)} %get-tuple-element.4) | data formatting | bytes 1032192
  93.9 1.9 %copy.11 = f32[7,48,384]{2,1,0:T(8,128)} copy(f32[7,48,384]{2,1,0:T(8,128)} %get-tuple-element.5) | data formatting | bytes 1032192

commit v3 on v2

--- a/solution.py
+++ b/solution.py
@@ -71,8 +71,19 @@
     return total
 
 
+def coded(value):
+    top = jnp.maximum(jnp.max(jnp.abs(value), axis=-2, keepdims=True), 1e-30)
+    code = jnp.round(value * (32767.0 / top)).astype(jnp.int32).astype(jnp.int16)
+    return code, top * (1.0 / 32767.0)
+
+
+def decoded(code, step):
+    return code.astype(jnp.int32).astype(jnp.float32) * step
+
+
 def kernel(groups, n_z, n_y, cap, rg, rs, psi, left, right, diag, sig_o, cor_o,
-           whole, lv, rv, dv, rsend, rrecv, part, yrecv, zacc, zrecv, sigv, corv,
+           whole, lv, rv, dv, rsend, rrecv, part, ycode, ystep, yrecv, ysrecv, zcode, zstep, zacc,
+           zrecv, zsrecv, sigv, corv,
            stat, statz, staty, statg, send_sem, recv_sem, local_sem):
     spg, rows, sec = psi.shape
     g = lax.axis_index("grp")
@@ -188,7 +199,8 @@
     across = []
 
     def y_out(j):
-        return remote(part.at[j, :, n_y - 1 - y], yrecv.at[j], y_peer)
+        return [remote(ystep.at[j], ysrecv.at[j], y_peer),
+                remote(ycode.at[j], yrecv.at[j], y_peer)]
 
     for j in range(spg):
         block = whole[j]
@@ -196,6 +208,7 @@
                                 preferred_element_type=jnp.float32).astype(jnp.bfloat16)
         value = jnp.dot(lv[j], image, preferred_element_type=jnp.float32)
         part[j] = value.reshape(n_z, n_y, rows, sec)
+        ycode[j], ystep[j] = coded(part[j, :, n_y - 1 - y])
         corr = corr + fold(block.astype(jnp.float32) * value)
         if j < AHEAD:
             across.append(y_out(j))
@@ -228,7 +241,7 @@
             copy.wait_recv()
         sigma = zacc[j, z]
         for d in range(1, n_z):
-            sigma = sigma + zrecv[j, d - 1]
+            sigma = sigma + decoded(zrecv[j, d - 1], zsrecv[j, d - 1])
         sigv[j] = sigma
         outs.append(local(sigv.at[j], sig_o.at[j]))
         wave = whole[j, rows_of(o), :].astype(jnp.float32)
@@ -238,7 +251,8 @@
 
     done = 0
     for j in range(spg):
-        across[j].wait_recv()
+        for copy in across[j]:
+            copy.wait_recv()
         if j < 2:
             sums_in(j, sums)
             sums = sums_out(j + 1)
@@ -247,10 +261,14 @@
             theta = jnp.sum(stat[3, 0]) / jnp.sum(stat[3, 1])
         if j + AHEAD < spg:
             across.append(y_out(j + AHEAD))
-        for k in range(n_z):
-            zacc[j, k] = part[j, k, y] + yrecv[j, k]
-        along.append([remote(zacc.at[j, lax.rem(z + d, n_z)], zrecv.at[j, d - 1], z_peer(d))
-                      for d in range(1, n_z)])
+        total = part[j, :, y] + decoded(yrecv[j], ysrecv[j])
+        zacc[j] = total
+        zcode[j], zstep[j] = coded(total)
+        along.append([])
+        for d in range(1, n_z):
+            there = lax.rem(z + d, n_z)
+            along[j].append(remote(zstep.at[j, there], zsrecv.at[j, d - 1], z_peer(d)))
+            along[j].append(remote(zcode.at[j, there], zrecv.at[j, d - 1], z_peer(d)))
         if j > LATE:
             finish(done)
             done += 1
@@ -269,9 +287,9 @@
     n_z = lax.axis_size("ops") // n_y
     spg, rows, sec = psi.shape
     cap = (spg + groups - 1) // groups
-    f32, bf16 = jnp.float32, jnp.bfloat16
+    f32, bf16, i16 = jnp.float32, jnp.bfloat16, jnp.int16
     cuts = len(chunks_of(spg))
-    copies = cuts * (2 * n_z - 1) + (groups - 1) * cap + spg * n_z + (n_z - 1) + 1 + (groups - 1)
+    copies = cuts * (2 * n_z - 1) + (groups - 1) * cap + 2 * spg * n_z + (n_z - 1) + 1 + (groups - 1)
     shape = jax.ShapeDtypeStruct((spg, rows, sec), f32)
     return pl.pallas_call(
         functools.partial(kernel, groups, n_z, n_y, cap),
@@ -286,9 +304,15 @@
             pltpu.VMEM(((groups - 1) * cap, sec, sec), bf16),
             pltpu.VMEM((groups * cap, sec, sec), bf16),
             pltpu.VMEM((spg, n_z, n_y, rows, sec), f32),
+            pltpu.VMEM((spg, n_z, rows, sec), i16),
+            pltpu.VMEM((spg, n_z, 1, sec), f32),
+            pltpu.VMEM((spg, n_z, rows, sec), i16),
+            pltpu.VMEM((spg, n_z, 1, sec), f32),
+            pltpu.VMEM((spg, n_z, rows, sec), i16),
+            pltpu.VMEM((spg, n_z, 1, sec), f32),
             pltpu.VMEM((spg, n_z, rows, sec), f32),
-            pltpu.VMEM((spg, n_z, rows, sec), f32),
-            pltpu.VMEM((spg, n_z - 1, rows, sec), f32),
+            pltpu.VMEM((spg, n_z - 1, rows, sec), i16),
+            pltpu.VMEM((spg, n_z - 1, 1, sec), f32),
             pltpu.VMEM((spg, rows, sec), f32),
             pltpu.VMEM((spg, rows, sec), f32),
             pltpu.VMEM((4, 2, 8, 128), f32),

time: 96 us -> 75.9 us (0.79)
  Pallas kernels: 91.4 us -> 71.4 us
    pallas_call x1, Pallas kernels: 91.4 us -> 71.4 us  [fused_shards(): pl.pallas_call(functools.partial(kernel, groups, n_z, n_y, cap), out_shap...]
where the time goes in v3:
time: 75.9 us; the launch traced here: 75.7 us
  Pallas kernels  71.4 us (94%)
  local copies, waits for them, and re-layouts  3.72 us (5%)
    pallas_call x1, Pallas kernels, fused_shards(): pl.pallas_call(functools.partial(kernel, groups, n_z, n_y, cap), out_shap...  71.4 us
    unnamed x2, local copies, waits for them, and re-layouts  3.72 us

profile of v3, /device:TPU:0, one launch (start us, length us, event | category | flops | bytes accessed | tf_op | source)
XLA Modules:
  0.0 75.7 jit_solution(15752204470373866067)
XLA Ops:
  0.6 71.4 %shard_map.77 = (f32[7,48,384]{2,1,0:T(8,128)}, f32[7,48,384]{2,1,0:T(8,128)}) custom-call(s32[28]{0:T(128)} %bitcast.1, s32[28]{0:T(128)} %rs.1, bf16[7,48,384]{2,1,0:T(8,128)(2,1)} %psi.1, bf16[7,1,384,384]{3,2,1,0:T(8,128)(2,1)} %left.1, bf16[7,1,384,384]{3,2,1,0:T(8,128)(2,1)} %right.1, f32[7,48,384]{2,1,0:T(8,128)} %diag.1), custom_call_target="tpu_custom_call" | custom-call | tf_op jit(solution)/shard_map/pallas_call | solution.py:294
  72.0 1.9 %copy.10 = f32[7,48,384]{2,1,0:T(8,128)} copy(f32[7,48,384]{2,1,0:T(8,128)} %get-tuple-element.4) | data formatting | bytes 1032192
  73.9 1.9 %copy.11 = f32[7,48,384]{2,1,0:T(8,128)} copy(f32[7,48,384]{2,1,0:T(8,128)} %get-tuple-element.5) | data formatting | bytes 1032192

commit v4 on v3

--- a/solution.py
+++ b/solution.py
@@ -53,10 +53,19 @@
     return (sigma, correction)
 
 
+def correct(sums, sigma, psi, diag, sig_o, cor_o):
+    theta = jnp.sum(sums[0]) / jnp.sum(sums[1])
+    for j in range(sigma.shape[0]):
+        value = sigma[j]
+        sig_o[j] = value
+        gap = diag[j] - theta
+        cor_o[j] = (value - theta * psi[j].astype(jnp.float32)) * gap / (gap * gap + 1.0)
+
+
 def chunks_of(spg):
     cuts, at = [], 0
     while at < spg:
-        size = min(2, spg - at) if spg - at != 3 else 3
+        size = 2 if spg - at > 3 else 1
         cuts.append((at, size))
         at += size
     return cuts
@@ -71,8 +80,8 @@
     return total
 
 
-def coded(value):
-    top = jnp.maximum(jnp.max(jnp.abs(value), axis=-2, keepdims=True), 1e-30)
+def coded(value, axes):
+    top = jnp.maximum(jnp.max(jnp.abs(value), axis=axes, keepdims=True), 1e-30)
     code = jnp.round(value * (32767.0 / top)).astype(jnp.int32).astype(jnp.int16)
     return code, top * (1.0 / 32767.0)
 
@@ -81,9 +90,9 @@
     return code.astype(jnp.int32).astype(jnp.float32) * step
 
 
-def kernel(groups, n_z, n_y, cap, rg, rs, psi, left, right, diag, sig_o, cor_o,
-           whole, lv, rv, dv, rsend, rrecv, part, ycode, ystep, yrecv, ysrecv, zcode, zstep, zacc,
-           zrecv, zsrecv, sigv, corv,
+def kernel(groups, n_z, n_y, cap, rg, rs, psi, left, right, sig_o, sums_o,
+           whole, lv, rv, rsend, rrecv, part, ycode, ystep, yrecv, ysrecv, zcode, zstep, zacc,
+           zrecv, zsrecv, sigv,
            stat, statz, staty, statg, send_sem, recv_sem, local_sem):
     spg, rows, sec = psi.shape
     g = lax.axis_index("grp")
@@ -128,7 +137,6 @@
     right_in = local(right.at[:, 0], rv)
     psi_in = local(psi, whole.at[:, rows_of(o)])
     left_in = local(left.at[:, 0], lv)
-    diag_in = local(diag, dv)
 
     barrier = pltpu.get_barrier_semaphore()
     peers = [z_peer(d) for d in range(1, n_z)] + [y_peer] + [g_peer(d) for d in range(1, groups)]
@@ -208,7 +216,7 @@
                                 preferred_element_type=jnp.float32).astype(jnp.bfloat16)
         value = jnp.dot(lv[j], image, preferred_element_type=jnp.float32)
         part[j] = value.reshape(n_z, n_y, rows, sec)
-        ycode[j], ystep[j] = coded(part[j, :, n_y - 1 - y])
+        ycode[j], ystep[j] = coded(part[j, :, n_y - 1 - y], (0, 1))
         corr = corr + fold(block.astype(jnp.float32) * value)
         if j < AHEAD:
             across.append(y_out(j))
@@ -231,10 +239,8 @@
         stat[stage + 1] = total
 
     sums = sums_out(0)
-    diag_in.wait()
     along = []
     outs = []
-    theta = None
 
     def finish(j):
         for copy in along[j]:
@@ -244,26 +250,19 @@
             sigma = sigma + decoded(zrecv[j, d - 1], zsrecv[j, d - 1])
         sigv[j] = sigma
         outs.append(local(sigv.at[j], sig_o.at[j]))
-        wave = whole[j, rows_of(o), :].astype(jnp.float32)
-        gap = dv[j] - theta
-        corv[j] = (sigma - theta * wave) * gap / (gap * gap + 1.0)
-        outs.append(local(corv.at[j], cor_o.at[j]))
 
     done = 0
     for j in range(spg):
         for copy in across[j]:
             copy.wait_recv()
-        if j < 2:
-            sums_in(j, sums)
-            sums = sums_out(j + 1)
-        elif j == LATE:
-            sums_in(2, sums)
-            theta = jnp.sum(stat[3, 0]) / jnp.sum(stat[3, 1])
+        if j in (1, 3):
+            sums_in(j // 2, sums)
+            sums = sums_out(j // 2 + 1)
         if j + AHEAD < spg:
             across.append(y_out(j + AHEAD))
         total = part[j, :, y] + decoded(yrecv[j], ysrecv[j])
         zacc[j] = total
-        zcode[j], zstep[j] = coded(total)
+        zcode[j], zstep[j] = coded(total, (1,))
         along.append([])
         for d in range(1, n_z):
             there = lax.rem(z + d, n_z)
@@ -272,6 +271,8 @@
         if j > LATE:
             finish(done)
             done += 1
+    sums_in(2, sums)
+    outs.append(local(stat.at[3], sums_o))
     while done < spg:
         finish(done)
         done += 1
@@ -291,29 +292,27 @@
     cuts = len(chunks_of(spg))
     copies = cuts * (2 * n_z - 1) + (groups - 1) * cap + 2 * spg * n_z + (n_z - 1) + 1 + (groups - 1)
     shape = jax.ShapeDtypeStruct((spg, rows, sec), f32)
-    return pl.pallas_call(
+    sigma, sums = pl.pallas_call(
         functools.partial(kernel, groups, n_z, n_y, cap),
-        out_shape=(shape, shape),
-        in_specs=[pl.BlockSpec(memory_space=pltpu.SMEM)] * 2 + [pl.BlockSpec(memory_space=pl.ANY)] * 4,
+        out_shape=(shape, jax.ShapeDtypeStruct((2, 8, 128), f32)),
+        in_specs=[pl.BlockSpec(memory_space=pltpu.SMEM)] * 2 + [pl.BlockSpec(memory_space=pl.ANY)] * 3,
         out_specs=(pl.BlockSpec(memory_space=pl.ANY),) * 2,
         scratch_shapes=[
             pltpu.VMEM((spg, sec, sec), bf16),
             pltpu.VMEM((spg, sec, sec), bf16),
             pltpu.VMEM((spg, sec, sec), bf16),
-            pltpu.VMEM((spg, rows, sec), f32),
             pltpu.VMEM(((groups - 1) * cap, sec, sec), bf16),
             pltpu.VMEM((groups * cap, sec, sec), bf16),
             pltpu.VMEM((spg, n_z, n_y, rows, sec), f32),
             pltpu.VMEM((spg, n_z, rows, sec), i16),
-            pltpu.VMEM((spg, n_z, 1, sec), f32),
+            pltpu.VMEM((spg, 1, 1, sec), f32),
             pltpu.VMEM((spg, n_z, rows, sec), i16),
-            pltpu.VMEM((spg, n_z, 1, sec), f32),
+            pltpu.VMEM((spg, 1, 1, sec), f32),
             pltpu.VMEM((spg, n_z, rows, sec), i16),
             pltpu.VMEM((spg, n_z, 1, sec), f32),
             pltpu.VMEM((spg, n_z, rows, sec), f32),
             pltpu.VMEM((spg, n_z - 1, rows, sec), i16),
             pltpu.VMEM((spg, n_z - 1, 1, sec), f32),
-            pltpu.VMEM((spg, rows, sec), f32),
             pltpu.VMEM((spg, rows, sec), f32),
             pltpu.VMEM((4, 2, 8, 128), f32),
             pltpu.VMEM((n_z - 1, 2, 8, 128), f32),
@@ -325,7 +324,13 @@
         ],
         compiler_params=pltpu.CompilerParams(
             collective_id=0, has_side_effects=True, vmem_limit_bytes=VMEM_BYTES),
-    )(right_group.reshape(-1), right_slot, psi, left_ops, right_ops, precond_diag)
+    )(right_group.reshape(-1), right_slot, psi, left_ops, right_ops)
+    return pl.pallas_call(
+        correct,
+        out_shape=(shape, shape),
+        in_specs=[pl.BlockSpec(memory_space=pltpu.VMEM)] * 4,
+        out_specs=(pl.BlockSpec(memory_space=pltpu.VMEM),) * 2,
+    )(sums, sigma, psi, precond_diag)
 
 
 def shards(psi, left_ops, right_ops, right_group, right_slot, precond_diag):

time: 75.9 us -> 71.5 us (0.942)
  local copies, waits for them, and re-layouts: 3.72 us -> 0 us
    unnamed x2 -> x0, local copies, waits for them, and re-layouts: 3.72 us -> none
    pallas_call x1, Pallas kernels: 71.4 us -> 68.2 us  [fused_shards(): pl.pallas_call(functools.partial(kernel, groups, n_z, n_y, cap), out_shap...]
    pallas_call x0 -> x1, Pallas kernels: none -> 2.47 us  [fused_shards(): pl.pallas_call(correct, out_shape=(shape, shape), in_specs=[pl.BlockSpec(...]
where the time goes in v4:
time: 71.5 us; the launch traced here: 71.3 us
  Pallas kernels  70.7 us (99%)
    pallas_call x1, Pallas kernels, fused_shards(): pl.pallas_call(functools.partial(kernel, groups, n_z, n_y, cap), out_shap...  68.2 us
    pallas_call x1, Pallas kernels, fused_shards(): pl.pallas_call(correct, out_shape=(shape, shape), in_specs=[pl.BlockSpec(...  2.47 us

profile of v4, /device:TPU:0, one launch (start us, length us, event | category | flops | bytes accessed | tf_op | source)
XLA Modules:
  0.0 71.3 jit_solution(9862100353821197201)
XLA Ops:
  0.6 68.2 %shard_map.77 = (f32[7,48,384]{2,1,0:T(8,128)}, f32[2,8,128]{2,1,0:T(8,128)}) custom-call(s32[28]{0:T(128)} %bitcast.1, s32[28]{0:T(128)} %rs.1, bf16[7,48,384]{2,1,0:T(8,128)(2,1)} %psi.3, bf16[7,1,384,384]{3,2,1,0:T(8,128)(2,1)} %left.1, bf16[7,1,384,384]{3,2,1,0:T(8,128)(2,1)} %right.1), custom_call_target="tpu_custom_call" | custom-call | tf_op jit(solution)/shard_map/pallas_call | solution.py:295
  68.8 2.5 %shard_map.78 = (f32[7,48,384]{2,1,0:T(8,128)}, f32[7,48,384]{2,1,0:T(8,128)}) custom-call(f32[2,8,128]{2,1,0:T(8,128)} %get-tuple-element.4.sums, f32[7,48,384]{2,1,0:T(8,128)} %get-tuple-element.5.sigma, bf16[7,48,384]{2,1,0:T(8,128)(2,1)} %psi.3, f32[7,48,384]{2,1,0:T(8,128)} %diag.1), custom_call_target="tpu_custom_call" | custom-call | tf_op jit(solution)/shard_map/pallas_call | solution.py:328
